TPU v7x, 32 devices: a whole 2x2x4 slice. The times are simulated.
32 devices in a mesh: layer: 4 (over x, core), row: 4 (over z), col: 2 (over y).
Axes of the slice: x: 2, y: 2, z: 4, core: 2. Of those that a mesh axis runs over, the one named last changes fastest.
Arguments:
- sources: bfloat16 [4, 96, 12288], P('layer', 'col', 'row'), may hold values from -6 to 6
- transmission: bfloat16 [4, 12288, 12288], P('layer', 'row', 'col'), may hold values from -0.0546875 to 0.0546875
- reflection: bfloat16 [4, 12288, 12288], P('layer', 'row', 'col'), may hold values from -0.02734375 to 0.02734375
Outputs:
- upgoing: bfloat16 [4, 96, 12288], P('layer', 'col', 'row')
All inputs are finite; a program needn't handle non-finite values.
Results may differ from a plain program's by a relative error of at most 0.012.
Values may be sent and summed in bfloat16 or wider, within the bound.
A program may use at most 128 MiB of HBM per device.

v0:
```python
import jax
import jax.numpy as jnp
from jax import lax
from jax.sharding import PartitionSpec as P


def from_root(array, axis, root):
    mine = lax.axis_index(axis) == root
    return lax.psum(jnp.where(mine, array, jnp.zeros_like(array)), axis)


def passed_along(array, axis, by):
    length = lax.axis_size(axis)
    pairs = [(i, i + by) for i in range(length) if 0 <= i + by < length]
    return lax.ppermute(array, axis, pairs)


def widen(narrow_traces, col_index, row_ratio):
    pieces = []
    for half in range(row_ratio):
        pieces.append(from_root(narrow_traces, "row", row_ratio * col_index + half))
    return jnp.concatenate(pieces, axis=1)


def shrink(wide_traces, row_index, row_ratio, row_width):
    own_part = lax.dynamic_slice_in_dim(
        wide_traces, row_index % row_ratio * row_width, row_width, 1
    )
    return from_root(own_part, "col", row_index // row_ratio)


def per_device(sources, transmission, reflection):
    layer_count = lax.axis_size("layer")
    row_ratio = lax.axis_size("row") // lax.axis_size("col")
    row_index = lax.axis_index("row")
    col_index = lax.axis_index("col")
    layer_index = lax.axis_index("layer")
    trans_tile = transmission[0]
    reflect_tile = reflection[0]
    row_width = trans_tile.shape[0]
    col_width = trans_tile.shape[1]
    source_narrow = lax.all_gather(sources[0], "col", axis=0, tiled=True)
    source_wide = widen(source_narrow, col_index, row_ratio)
    trace_count = source_narrow.shape[0]
    incoming_wide = jnp.zeros((trace_count, col_width), jnp.bfloat16)
    incoming_narrow = jnp.zeros((trace_count, row_width), jnp.bfloat16)
    incident_wide = source_wide
    down_wide = incoming_wide
    for step in range(layer_count):
        incident_narrow = (
            incoming_narrow.astype(jnp.float32) + source_narrow.astype(jnp.float32)
        ).astype(jnp.bfloat16)
        partial_value = jnp.dot(incident_narrow, trans_tile, preferred_element_type=jnp.float32)
        down_wide = lax.psum(partial_value, "row").astype(jnp.bfloat16)
        incoming_narrow = passed_along(
            shrink(down_wide, row_index, row_ratio, row_width), "layer", 1
        )
        if step == layer_count - 1:
            incident_wide = widen(incident_narrow, col_index, row_ratio)
    contract = (((1,), (1,)), ((), ()))
    upward_wide = down_wide
    result = None
    for step in range(layer_count):
        passed = lax.dot_general(
            upward_wide, trans_tile, contract, preferred_element_type=jnp.float32
        )
        bounced = lax.dot_general(
            incident_wide, reflect_tile, contract, preferred_element_type=jnp.float32
        )
        result = lax.psum_scatter(passed + bounced, "col", scatter_dimension=0, tiled=True).astype(
            jnp.bfloat16
        )
        if step < layer_count - 1:
            gathered = lax.all_gather(result, "col", axis=0, tiled=True)
            arrived = widen(passed_along(gathered, "layer", -1), col_index, row_ratio)
            upward_wide = jnp.where(layer_index == layer_count - 1, down_wide, arrived)
    return result[None]


def solution(mesh):
    return jax.shard_map(
        per_device,
        mesh=mesh,
        in_specs=(P("layer", "col", "row"), P("layer", "row", "col"), P("layer", "row", "col")),
        out_specs=P("layer", "col", "row"),
        check_vma=False,
    )
```

profile of v0, /device:TPU:0, one launch (start us, length us, event | category | flops | bytes accessed | tf_op | source)
XLA Modules:
  0.0 978.6 jit_solution(17951817777036338590)
XLA Ops:
  6.5 10.9 %all-gather = bf16[1,96,3072]{2,1,0:T(8,128)(2,1)S(1)} all-gather(bf16[1,48,3072]{2,1,0:T(8,128)(2,1)} %param.3), channel_id=2, replica_groups=mesh['layer'=4,'row'=4,'col'=2] {'col'}, dimensions={1}, use_global_device_ids=true | all-gather | bytes 884736 | tf_op jit(solution)/shard_map/all_gather | solution.py:42
  17.5 14.9 %fusion.16 = f32[96,6144]{1,0:T(8,128)S(1)} fusion(bf16[1,3072,6144]{2,1,0:T(8,128)(2,1)} %param.4, bf16[1,96,3072]{2,1,0:T(8,128)(2,1)S(1)} %all-gather), kind=kOutput, calls=%fused_computation.16 | convolution fusion | flops 3623878656 | bytes 40697856 | tf_op jit(solution)/shard_map/dot_general | solution.py:53
  32.3 85.1 %all-reduce.29 = bf16[96,6144]{1,0:T(8,128)(2,1)} all-reduce(f32[96,6144]{1,0:T(8,128)S(1)} %fusion.16), channel_id=1, replica_groups=mesh['layer'=4,'row'=4,'col'=2] {'row'}, use_global_device_ids=true, to_apply=%region_0.0 | all-reduce | flops 589824 | bytes 3538944 | tf_op jit(solution)/shard_map/psum | solution.py:54
  119.6 29.3 %all-reduce.16.cloned.1.call-done = bf16[96,3072]{1,0:T(8,128)(2,1)} async-done(((bf16[96,3072]{1,0:T(8,128)(2,1)}), bf16[96,3072]{1,0:T(8,128)(2,1)}) %all-reduce.16.cloned.1.call-update) | async-done | bytes 589840 | tf_op jit(solution)/shard_map/psum | solution.py:9
  152.3 14.9 %fusion.14 = f32[96,6144]{1,0:T(8,128)S(1)} fusion(bf16[1,3072,6144]{2,1,0:T(8,128)(2,1)} %param.4, bf16[96,3072]{1,0:T(8,128)(2,1)S(1)} %collective-permute-done, bf16[1,96,3072]{2,1,0:T(8,128)(2,1)S(1)} %all-gather), kind=kOutput, calls=%fused_computation.14 | convolution fusion | flops 3625058304 | bytes 41287680 | tf_op jit(solution)/shard_map/dot_general | solution.py:53
  167.2 80.2 %all-reduce.30 = bf16[96,6144]{1,0:T(8,128)(2,1)} all-reduce(f32[96,6144]{1,0:T(8,128)S(1)} %fusion.14), channel_id=1, replica_groups=mesh['layer'=4,'row'=4,'col'=2] {'row'}, use_global_device_ids=true, to_apply=%region_2.3 | all-reduce | flops 589824 | bytes 3538944 | tf_op jit(solution)/shard_map/psum | solution.py:54
  249.4 34.7 %all-reduce.18.cloned.1.call-done = bf16[96,3072]{1,0:T(8,128)(2,1)} async-done(((bf16[96,3072]{1,0:T(8,128)(2,1)}), bf16[96,3072]{1,0:T(8,128)(2,1)}) %all-reduce.18.cloned.1.call-update) | async-done | bytes 589840 | tf_op jit(solution)/shard_map/psum | solution.py:9
  287.6 14.9 %fusion.12 = f32[96,6144]{1,0:T(8,128)S(1)} fusion(bf16[1,3072,6144]{2,1,0:T(8,128)(2,1)} %param.4, bf16[96,3072]{1,0:T(8,128)(2,1)S(1)} %collective-permute-done.1, bf16[1,96,3072]{2,1,0:T(8,128)(2,1)S(1)} %all-gather), kind=kOutput, calls=%fused_computation.12 | convolution fusion | flops 3625058304 | bytes 41287680 | tf_op jit(solution)/shard_map/dot_general | solution.py:53
  302.5 80.2 %all-reduce.31 = bf16[96,6144]{1,0:T(8,128)(2,1)} all-reduce(f32[96,6144]{1,0:T(8,128)S(1)} %fusion.12), channel_id=1, replica_groups=mesh['layer'=4,'row'=4,'col'=2] {'row'}, use_global_device_ids=true, to_apply=%region_4.5 | all-reduce | flops 589824 | bytes 3538944 | tf_op jit(solution)/shard_map/psum | solution.py:54
  384.7 34.7 %all-reduce.20.cloned.1.call-done = bf16[96,3072]{1,0:T(8,128)(2,1)} async-done(((bf16[96,3072]{1,0:T(8,128)(2,1)}), bf16[96,3072]{1,0:T(8,128)(2,1)}) %all-reduce.20.cloned.1.call-update) | async-done | bytes 589840 | tf_op jit(solution)/shard_map/psum | solution.py:9
  422.8 14.9 %fusion.10 = f32[96,6144]{1,0:T(8,128)S(1)} fusion(bf16[1,3072,6144]{2,1,0:T(8,128)(2,1)} %param.4, bf16[96,3072]{1,0:T(8,128)(2,1)S(1)} %collective-permute-done.2, bf16[1,96,3072]{2,1,0:T(8,128)(2,1)S(1)} %all-gather), kind=kOutput, calls=%fused_computation.10 | convolution fusion | flops 3625058304 | bytes 41287680 | tf_op jit(solution)/shard_map/dot_general | solution.py:53
  439.1 117.6 %all-reduce.32 = bf16[96,6144]{1,0:T(8,128)(2,1)S(1)} all-reduce(f32[96,6144]{1,0:T(8,128)S(1)} %fusion.10), channel_id=1, replica_groups=mesh['layer'=4,'row'=4,'col'=2] {'row'}, use_global_device_ids=true, to_apply=%region_6.7 | all-reduce | flops 589824 | bytes 3538944 | tf_op jit(solution)/shard_map/psum | solution.py:54
  556.7 17.4 %fusion = f32[96,3072]{1,0:T(8,128)S(1)} fusion(bf16[1,3072,6144]{2,1,0:T(8,128)(2,1)} %param.5, bf16[96,3072]{1,0:T(8,128)(2,1)} %get-tuple-element.11, bf16[96,3072]{1,0:T(8,128)(2,1)} %get-tuple-element.12), kind=kOutput, calls=%fused_computation | convolution fusion | flops 3626237952 | bytes 40108032 | tf_op jit(solution)/shard_map/dot_general | solution.py:67
  574.1 18.2 %fusion.18 = f32[96,3072]{1,0:T(8,128)} fusion(f32[96,3072]{1,0:T(8,128)S(1)} %fusion, bf16[96,6144]{1,0:T(8,128)(2,1)S(1)} %all-reduce.32, bf16[1,3072,6144]{2,1,0:T(8,128)(2,1)} %param.4), kind=kOutput, calls=%fused_computation.18 | convolution fusion | flops 3624173568 | bytes 41287680 | tf_op jit(solution)/shard_map/dot_general | solution.py:64
  592.3 26.5 %reduce-scatter.5.cloned.1.call-done = f32[48,3072]{1,0:T(8,128)} async-done(((f32[96,3072]{1,0:T(8,128)}), f32[48,3072]{1,0:T(8,128)}) %reduce-scatter.5.cloned.1.call-update) | async-done | bytes 589840 | tf_op jit(solution)/shard_map/reduce_scatter | solution.py:70
  634.5 61.8 %all-reduce.26.cloned.1.call-done = (bf16[96,3072]{1,0:T(8,128)(2,1)}, bf16[96,3072]{1,0:T(8,128)(2,1)}) async-done(((bf16[96,3072]{1,0:T(8,128)(2,1)}, bf16[96,3072]{1,0:T(8,128)(2,1)}), (bf16[96,3072]{1,0:T(8,128)(2,1)}, bf16[96,3072]{1,0:T(8,128)(2,1)})) %all-reduce.26.cloned.1.call-update) | async-done | bytes 1179664 | tf_op jit(solution)/shard_map/psum | solution.py:9
  696.3 18.3 %fusion.21 = f32[96,3072]{1,0:T(8,128)} fusion(f32[96,3072]{1,0:T(8,128)S(1)} %fusion, bf16[1,3072,6144]{2,1,0:T(8,128)(2,1)} %param.4, bf16[96,6144]{1,0:T(8,128)(2,1)S(1)} %all-reduce.32, bf16[96,3072]{1,0:T(8,128)(2,1)} %get-tuple-element.9, bf16[96,3072]{1,0:T(8,128)(2,1)} %get-tuple-element.10, pred[]{:T(512)S(6)} %eq.12), kind=kOutput, calls=%fused_computation.19 | convolution fusion | flops 3627122688 | bytes 42467328 | tf_op jit(solution)/shard_map/dot_general | solution.py:64
  714.6 21.3 %reduce-scatter.7.cloned.1.call-done = f32[48,3072]{1,0:T(8,128)} async-done(((f32[96,3072]{1,0:T(8,128)}), f32[48,3072]{1,0:T(8,128)}) %reduce-scatter.7.cloned.1.call-update) | async-done | bytes 589840 | tf_op jit(solution)/shard_map/reduce_scatter | solution.py:70
  751.4 62.0 %all-reduce.24.cloned.1.call-done = (bf16[96,3072]{1,0:T(8,128)(2,1)}, bf16[96,3072]{1,0:T(8,128)(2,1)}) async-done(((bf16[96,3072]{1,0:T(8,128)(2,1)}, bf16[96,3072]{1,0:T(8,128)(2,1)}), (bf16[96,3072]{1,0:T(8,128)(2,1)}, bf16[96,3072]{1,0:T(8,128)(2,1)})) %all-reduce.24.cloned.1.call-update) | async-done | bytes 1179664 | tf_op jit(solution)/shard_map/psum | solution.py:9
  813.4 18.3 %fusion.24 = f32[96,3072]{1,0:T(8,128)} fusion(f32[96,3072]{1,0:T(8,128)S(1)} %fusion, bf16[1,3072,6144]{2,1,0:T(8,128)(2,1)} %param.4, bf16[96,6144]{1,0:T(8,128)(2,1)S(1)} %all-reduce.32, bf16[96,3072]{1,0:T(8,128)(2,1)} %get-tuple-element.7, bf16[96,3072]{1,0:T(8,128)(2,1)} %get-tuple-element.8, pred[]{:T(512)S(6)} %eq.12), kind=kOutput, calls=%fused_computation.20 | convolution fusion | flops 3627122688 | bytes 42467328 | tf_op jit(solution)/shard_map/dot_general | solution.py:64
  831.8 21.3 %reduce-scatter.9.cloned.1.call-done = f32[48,3072]{1,0:T(8,128)} async-done(((f32[96,3072]{1,0:T(8,128)}), f32[48,3072]{1,0:T(8,128)}) %reduce-scatter.9.cloned.1.call-update) | async-done | bytes 589840 | tf_op jit(solution)/shard_map/reduce_scatter | solution.py:70
  868.5 62.0 %all-reduce.22.cloned.1.call-done = (bf16[96,3072]{1,0:T(8,128)(2,1)}, bf16[96,3072]{1,0:T(8,128)(2,1)}) async-done(((bf16[96,3072]{1,0:T(8,128)(2,1)}, bf16[96,3072]{1,0:T(8,128)(2,1)}), (bf16[96,3072]{1,0:T(8,128)(2,1)}, bf16[96,3072]{1,0:T(8,128)(2,1)})) %all-reduce.22.cloned.1.call-update) | async-done | bytes 1179664 | tf_op jit(solution)/shard_map/psum | solution.py:9
  930.6 18.3 %fusion.27 = f32[96,3072]{1,0:T(8,128)} fusion(f32[96,3072]{1,0:T(8,128)S(1)} %fusion, bf16[1,3072,6144]{2,1,0:T(8,128)(2,1)} %param.4, bf16[96,6144]{1,0:T(8,128)(2,1)S(1)} %all-reduce.32, bf16[96,3072]{1,0:T(8,128)(2,1)} %get-tuple-element.5, bf16[96,3072]{1,0:T(8,128)(2,1)} %get-tuple-element.6, pred[]{:T(512)S(6)} %eq.12), kind=kOutput, calls=%fused_computation.21 | convolution fusion | flops 3627122688 | bytes 42467328 | tf_op jit(solution)/shard_map/dot_general | solution.py:64
  948.9 21.4 %reduce-scatter.11.cloned.1.call-done = f32[48,3072]{1,0:T(8,128)} async-done(((f32[96,3072]{1,0:T(8,128)}), f32[48,3072]{1,0:T(8,128)}) %reduce-scatter.11.cloned.1.call-update) | async-done | bytes 589840 | tf_op jit(solution)/shard_map/reduce_scatter | solution.py:70
  (49 shorter events, 66.1 us)
Async XLA Ops:
  6.5 142.3 %all-reduce.16.cloned.1.call-start = ((), (), s32[]{:S(2)}) async-start(), calls=%async_computation.4 | async-start | bytes 1179648 | tf_op jit(solution)/shard_map/psum | solution.py:9
  119.5 164.6 %all-reduce.18.cloned.1.call-start = ((), (), s32[]{:S(2)}) async-start(), calls=%async_computation.5 | async-start | bytes 1179648 | tf_op jit(solution)/shard_map/psum | solution.py:9
  148.9 3.4 collective-permute-start
  249.4 170.1 %all-reduce.20.cloned.1.call-start = ((), (), s32[]{:S(2)}) async-start(), calls=%async_computation.6 | async-start | bytes 1179648 | tf_op jit(solution)/shard_map/psum | solution.py:9
  284.2 3.4 collective-permute-start.1
  384.7 172.0 %all-reduce.28.cloned.1.call-start = ((), (), s32[]{:S(2)}) async-start(), calls=%async_computation.14 | async-start | bytes 2359296 | tf_op jit(solution)/shard_map/psum | solution.py:9
  419.4 3.4 collective-permute-start.2
  439.0 179.8 %reduce-scatter.5.cloned.1.call-start = ((), (), s32[]{:S(2)}) async-start(), calls=%async_computation.7 | async-start | bytes 1769472 | tf_op jit(solution)/shard_map/reduce_scatter | solution.py:70
  592.3 104.0 %all-reduce.26.cloned.1.call-start = ((), (), s32[]{:S(2)}) async-start(), calls=%async_computation.13 | async-start | bytes 2359296 | tf_op jit(solution)/shard_map/psum | solution.py:9
  629.2 3.9 collective-permute-start.3
  634.2 101.8 %reduce-scatter.7.cloned.1.call-start = ((), (), s32[]{:S(2)}) async-start(), calls=%async_computation.8 | async-start | bytes 1769472 | tf_op jit(solution)/shard_map/reduce_scatter | solution.py:70
  714.6 98.8 %all-reduce.24.cloned.1.call-start = ((), (), s32[]{:S(2)}) async-start(), calls=%async_computation.12 | async-start | bytes 2359296 | tf_op jit(solution)/shard_map/psum | solution.py:9
  746.3 3.9 collective-permute-start.4
  751.3 101.8 %reduce-scatter.9.cloned.1.call-start = ((), (), s32[]{:S(2)}) async-start(), calls=%async_computation.9 | async-start | bytes 1769472 | tf_op jit(solution)/shard_map/reduce_scatter | solution.py:70
  831.7 98.8 %all-reduce.22.cloned.1.call-start = ((), (), s32[]{:S(2)}) async-start(), calls=%async_computation.11 | async-start | bytes 2359296 | tf_op jit(solution)/shard_map/psum | solution.py:9
  863.4 3.9 collective-permute-start.5
  868.5 101.8 %reduce-scatter.11.cloned.1.call-start = ((), (), s32[]{:S(2)}) async-start(), calls=%async_computation.10 | async-start | bytes 1769472 | tf_op jit(solution)/shard_map/reduce_scatter | solution.py:70
Sparse Core Ops, SparseCore 0:
  119.6 29.1 all-reduce.15
  249.5 34.6 all-reduce.17
  384.8 34.5 all-reduce.19
  439.1 102.0 all-reduce.27
  592.4 26.3 reduce-scatter.4
  634.3 61.9 all-reduce.25
  714.7 21.2 reduce-scatter.6
  751.4 61.9 all-reduce.23
  831.8 21.2 reduce-scatter.8
  868.6 61.9 all-reduce.21
  949.0 21.2 reduce-scatter.10
where the time goes:
time: 979 us
  blocking collectives  402 us (41%)
  waiting for transfers between devices  388 us (40%)
  matrix products  150 us (15%)
  other arithmetic  15.7 us (2%)
  between operations  13.4 us (1%)
    psum x4, blocking collectives, per_device(): down_wide = lax.psum(partial_value, 'row').astype(jnp.bfloat16)  363 us
    psum x7, waiting for transfers between devices, from_root(): return lax.psum(jnp.where(mine, array, jnp.zeros_like(array)), axis)  285 us
    reduce_scatter x4, waiting for transfers between devices, per_device(): lax.psum_scatter(passed + bounced, 'col', scatter_dimension=0, tiled=True)  90.5 us
    dot_general x4, matrix products, per_device(): lax.dot_general(upward_wide, trans_tile, contract, preferred_element_type...  73.1 us
    dot_general x4, matrix products, per_device(): jnp.dot(incident_narrow, trans_tile, preferred_element_type=jnp.float32)  59.5 us
    all_gather x3, blocking collectives, per_device(): gathered = lax.all_gather(result, 'col', axis=0, tiled=True)  27.7 us
  transfers between devices with their start and end apart: 17, of which 16 were waited for; matrix products, arithmetic and copies ran while one was open for 0% of the time, Pallas kernels for 0%

commit v1 on v0

v1 whole, which is shorter than its diff:
```python
import functools

import jax
import jax.numpy as jnp
from jax import lax
from jax.experimental import pallas as pl
from jax.experimental.pallas import tpu as pltpu
from jax.sharding import PartitionSpec as P

MESH = pl.DeviceIdType.MESH
BF16 = jnp.bfloat16
F32 = jnp.float32


def kernel(
    layers, rows, cols, pieces, r_tile,
    src_ref, trans_ref, refl_ref, out_ref,
    tv, rbuf, sall, nin, incn, pbuf, ybuf, zbuf, nat, ginc, gup, acc, ubuf, urec, upnat,
    t_sem, r_sem, s_send, s_recv, n_send, n_recv, y_send, y_recv, z_send, z_recv,
    g1_send, g1_recv, g2_send, g2_recv, u_send, u_recv, v_send, v_recv,
):
    ratio = rows // cols
    chunks = ratio * pieces
    lay, row, col = (lax.axis_index(name) for name in ("layer", "row", "col"))
    part, cw = nat.shape[1], nat.shape[2]
    traces = cols * part
    r_count = refl_ref.shape[0] // r_tile
    last = layers - 1

    def other(index, by, size):
        return lax.rem(index + by, size)

    def remote(src, dst, send, recv, target):
        return pltpu.make_async_remote_copy(
            src_ref=src, dst_ref=dst, send_sem=send, recv_sem=recv,
            device_id=target, device_id_type=MESH,
        )

    def t_copy(j):
        start = pl.multiple_of(j * cw, 128)
        return pltpu.make_async_copy(trans_ref.at[:, pl.ds(start, cw)], tv.at[j], t_sem.at[j])

    def r_copy(i, slot):
        start = pl.multiple_of(i * r_tile, 16)
        return pltpu.make_async_copy(
            refl_ref.at[pl.ds(start, r_tile), :], rbuf.at[slot], r_sem.at[slot]
        )

    def copy_src(c):
        return remote(src_ref, sall.at[col], s_send.at[c], s_recv.at[col], (lay, row, c))

    def got_src(c):
        return remote(src_ref, sall.at[c], s_send.at[c], s_recv.at[c], (lay, row, c))

    def copy_next(c, p):
        return remote(nat.at[p], nin.at[col, p], n_send.at[c, p], n_recv.at[col, p],
                      (lax.min(lay + 1, last), row, c))

    def got_next(c, p):
        return remote(nat.at[p], nin.at[c, p], n_send.at[c, p], n_recv.at[c, p],
                      (lax.max(lay - 1, 0), row, c))

    def copy_y(c, j):
        return remote(pbuf.at[j, c], ybuf.at[col, j], y_send.at[c, j], y_recv.at[col, j],
                      (lay, row, c))

    def got_y(c, j):
        return remote(pbuf.at[j, c], ybuf.at[c, j], y_send.at[c, j], y_recv.at[c, j],
                      (lay, row, c))

    def copy_z(c, j, own):
        block = pbuf.at[j, col] if own else ybuf.at[c, j]
        goal = ratio * c + lax.div(j, pieces)
        return goal, block, remote(
            block, zbuf.at[row, lax.rem(j, pieces)], z_send.at[c, j],
            z_recv.at[row, lax.rem(j, pieces)], (lay, goal, col),
        )

    def got_z(r, p):
        return remote(nat.at[p], zbuf.at[r, p], z_send.at[0, 0], z_recv.at[r, p],
                      (lay, r, col))

    def copy_g1(which, buf, r):
        return remote(buf.at[row, :, col], buf.at[row, :, col], g1_send.at[which, r],
                      g1_recv.at[which, row], (lay, r, col))

    def got_g1(which, buf, r):
        return remote(buf.at[r, :, col], buf.at[r, :, col], g1_send.at[which, r],
                      g1_recv.at[which, r], (lay, r, col))

    def copy_g2(which, buf, r):
        return remote(buf.at[r, :, col], buf.at[r, :, col], g2_send.at[which, r],
                      g2_recv.at[which, r, col], (lay, row, lax.div(r, ratio)))

    def got_g2(which, buf, r, c):
        return remote(buf.at[r, :, c], buf.at[r, :, c], g2_send.at[which, r],
                      g2_recv.at[which, r, c], (lay, row, c))

    def copy_u(c):
        return remote(ubuf.at[c], urec.at[col], u_send.at[c], u_recv.at[col], (lay, row, c))

    def got_u(c):
        return remote(ubuf.at[c], urec.at[c], u_send.at[c], u_recv.at[c], (lay, row, c))

    def copy_v():
        return remote(nat, upnat, v_send, v_recv, (lax.max(lay - 1, 0), row, col))

    def got_v():
        return remote(nat, upnat, v_send, v_recv, (lax.min(lay + 1, last), row, col))

    for j in range(chunks):
        t_copy(j).start()

    barrier = pltpu.get_barrier_semaphore()

    def greet(target):
        pl.semaphore_signal(barrier, inc=1, device_id=target, device_id_type=MESH)

    for d in range(1, rows):
        greet((lay, other(row, d, rows), col))
    for d in range(1, cols):
        greet((lay, row, other(col, d, cols)))

    @pl.when(lay > 0)
    def _():
        for c in range(cols):
            greet((lay - 1, row, c))

    @pl.when(lay < last)
    def _():
        for c in range(cols):
            greet((lay + 1, row, c))

    near = (lay > 0).astype(jnp.int32) + (lay < last).astype(jnp.int32)
    pl.semaphore_wait(barrier, rows + cols - 2 + cols * near)

    for d in range(1, cols):
        copy_src(other(col, d, cols)).start()
    sall[col] = src_ref[...]
    for d in range(1, cols):
        got_src(other(col, d, cols)).wait_recv()

    @pl.when(lay == 0)
    def _():
        for p in range(pieces):
            incn[p] = sall[:, p]

    @pl.when(lay > 0)
    def _():
        for p in range(pieces):
            for c in range(cols):
                got_next(c, p).wait_recv()
            incn[p] = (nin[:, p].astype(F32) + sall[:, p].astype(F32)).astype(BF16)

    for p in range(pieces):
        ginc[row, p, col] = incn[p, col]
    for d in range(1, rows):
        copy_g1(0, ginc, other(row, d, rows)).start()

    def to_row(c, j, own):
        goal, block, copy = copy_z(c, j, own)

        @pl.when(goal == row)
        def _():
            zbuf[row, lax.rem(j, pieces)] = block[...]

        @pl.when(goal != row)
        def _():
            copy.start()

    def forward(j):
        for d in range(1, cols):
            c = other(col, d, cols)
            got_y(c, j).wait_recv()
            to_row(c, j, False)

    def down_step(j, carry):
        t_copy(j).wait()
        total = jnp.zeros((traces, cw), F32)
        for p in range(pieces):
            total += jnp.dot(
                incn[p].reshape(traces, cw), tv[j, pl.ds(p * cw, cw), :],
                preferred_element_type=F32,
            )
        pbuf[j] = total.astype(BF16).reshape(cols, part, cw)
        for d in range(1, cols):
            copy_y(other(col, d, cols), j).start()
        to_row(col, j, True)

        @pl.when(j > 0)
        def _():
            forward(j - 1)

        return carry

    lax.fori_loop(0, chunks, down_step, 0)
    forward(chunks - 1)

    for p in range(pieces):
        for d in range(1, rows):
            got_z(other(row, d, rows), p).wait_recv()
        nat[p] = jnp.sum(zbuf[:, p].astype(F32), axis=0).astype(BF16)

        @pl.when(lay < last)
        def _():
            for c in range(cols):
                copy_next(c, p).start()

    def set_out(block):
        gup[row, :, col] = block[...]
        for d in range(1, rows):
            copy_g1(1, gup, other(row, d, rows)).start()

    @pl.when(lay == last)
    def _():
        set_out(nat)

    def spread(which, buf):
        for d in range(rows):
            r = other(row, d, rows)
            if d > 0:
                got_g1(which, buf, r).wait_recv()

            @pl.when(lax.div(r, ratio) != col)
            def _():
                copy_g2(which, buf, r).start()

    def complete(which, buf, b):
        for d in range(1, cols):
            got_g2(which, buf, ratio * col + b, other(col, d, cols)).wait_recv()

    contract = (((1,), (1,)), ((), ()))

    r_copy(0, 0).start()
    spread(0, ginc)
    for b in range(ratio):
        complete(0, ginc, b)

    def reflect_step(i, carry):
        slot = lax.rem(i, 2)
        r_copy(i, slot).wait()

        @pl.when(i + 1 < r_count)
        def _():
            r_copy(i + 1, 1 - slot).start()

        total = jnp.zeros((traces, r_tile), F32)
        for b in range(ratio):
            for p in range(pieces):
                total += lax.dot_general(
                    ginc[ratio * col + b, p].reshape(traces, cw),
                    rbuf[slot, :, pl.ds((b * pieces + p) * cw, cw)],
                    contract, preferred_element_type=F32,
                )
        acc[i] = total
        return carry

    lax.fori_loop(0, r_count, reflect_step, 0)

    @pl.when(lay < last)
    def _():
        got_v().wait_recv()
        set_out(upnat)

    spread(1, gup)

    def up_step(j, carry):
        lhs = gup[ratio * col + lax.div(j, pieces), lax.rem(j, pieces)].reshape(traces, cw)
        for i in range(r_count):
            acc[i] += lax.dot_general(
                lhs, tv[j, pl.ds(i * r_tile, r_tile), :], contract, preferred_element_type=F32
            )
        return carry

    for b in range(ratio):
        complete(1, gup, b)
        lax.fori_loop(b * pieces, (b + 1) * pieces, up_step, 0)

    per = cw // r_tile

    def piece_of(p, c):
        tiles = []
        for i in range(per):
            tiles.append(acc[p * per + i, pl.ds(pl.multiple_of(c * part, 8), part), :])
        return jnp.concatenate(tiles, axis=1)

    for d in range(1, cols):
        c = other(col, d, cols)
        for p in range(pieces):
            ubuf[c, p] = piece_of(p, c).astype(BF16)
        copy_u(c).start()

    @pl.when(lay < last)
    def _():
        for c in range(cols):
            for p in range(pieces):
                copy_next(c, p).wait_send()

    for d in range(1, cols):
        got_u(other(col, d, cols)).wait_recv()
    for p in range(pieces):
        total = piece_of(p, col)
        for d in range(1, cols):
            total += urec[other(col, d, cols), p].astype(F32)
        result = total.astype(BF16)
        nat[p] = result
        out_ref[:, p * cw:(p + 1) * cw] = result

    @pl.when(lay > 0)
    def _():
        copy_v().start()

    for d in range(1, cols):
        c = other(col, d, cols)
        copy_src(c).wait_send()
        copy_u(c).wait_send()
        for j in range(chunks):
            copy_y(c, j).wait_send()
    for d in range(cols):
        c = other(col, d, cols)
        for j in range(chunks):
            goal, _, copy = copy_z(c, j, d == 0)

            @pl.when(goal != row)
            def _():
                copy.wait_send()

    for which, buf in ((0, ginc), (1, gup)):
        for d in range(1, rows):
            copy_g1(which, buf, other(row, d, rows)).wait_send()
        for r in range(rows):
            @pl.when(r // ratio != col)
            def _():
                copy_g2(which, buf, r).wait_send()

    @pl.when(lay > 0)
    def _():
        copy_v().wait_send()


def split_of(width):
    for pieces in (4, 3, 2):
        if width % (pieces * 128) == 0:
            return pieces
    return 1


def per_device(layers, rows, cols, sources, transmission, reflection):
    ratio = rows // cols
    own, width = sources.shape[1], sources.shape[2]
    part = -(-own // 16) * 16
    pieces = split_of(width)
    cw = width // pieces
    chunks = ratio * pieces
    r_tile = 256 if cw % 256 == 0 else 128
    traces = cols * part
    src = jnp.pad(sources[0], ((0, part - own), (0, 0)))
    src = src.reshape(part, pieces, cw).transpose(1, 0, 2)
    dma, vmem = pltpu.SemaphoreType.DMA, pltpu.VMEM
    result = pl.pallas_call(
        functools.partial(kernel, layers, rows, cols, pieces, r_tile),
        out_shape=jax.ShapeDtypeStruct((part, width), BF16),
        in_specs=[
            pl.BlockSpec(memory_space=pltpu.VMEM),
            pl.BlockSpec(memory_space=pl.ANY),
            pl.BlockSpec(memory_space=pl.ANY),
        ],
        out_specs=pl.BlockSpec(memory_space=pltpu.VMEM),
        scratch_shapes=[
            vmem((chunks, width, cw), BF16),
            vmem((2, r_tile, ratio * width), BF16),
            vmem((cols, pieces, part, cw), BF16),
            vmem((cols, pieces, part, cw), BF16),
            vmem((pieces, cols, part, cw), BF16),
            vmem((chunks, cols, part, cw), BF16),
            vmem((cols, chunks, part, cw), BF16),
            vmem((rows, pieces, part, cw), BF16),
            vmem((pieces, part, cw), BF16),
            vmem((rows, pieces, cols, part, cw), BF16),
            vmem((rows, pieces, cols, part, cw), BF16),
            vmem((width // r_tile, traces, r_tile), F32),
            vmem((cols, pieces, part, cw), BF16),
            vmem((cols, pieces, part, cw), BF16),
            vmem((pieces, part, cw), BF16),
            dma((chunks,)), dma((2,)),
            dma((cols,)), dma((cols,)),
            dma((cols, pieces)), dma((cols, pieces)),
            dma((cols, chunks)), dma((cols, chunks)),
            dma((cols, chunks)), dma((rows, pieces)),
            dma((2, rows)), dma((2, rows)),
            dma((2, rows)), dma((2, rows, cols)),
            dma((cols,)), dma((cols,)),
            dma, dma,
        ],
        compiler_params=pltpu.CompilerParams(
            collective_id=0, has_side_effects=True, vmem_limit_bytes=66_000_000
        ),
    )(src, transmission[0], reflection[0])
    return result[None, :own]


def solution(mesh):
    sizes = [mesh.shape[name] for name in ("layer", "row", "col")]
    return jax.shard_map(
        functools.partial(per_device, *sizes),
        mesh=mesh,
        in_specs=(P("layer", "col", "row"), P("layer", "row", "col"), P("layer", "row", "col")),
        out_specs=P("layer", "col", "row"),
        check_vma=False,
    )
```

time: 979 us -> 307 us (0.31)
  blocking collectives: 402 us -> 0 us
  waiting for transfers between devices: 388 us -> 0 us
  Pallas kernels: 0 us -> 299 us
  matrix products: 150 us -> 0 us
  other arithmetic: 15.7 us -> 0 us
  between operations: 13.4 us -> 0.01 us
    psum x4 -> x0, blocking collectives: 363 us -> none  [per_device(): down_wide = lax.psum(partial_value, 'row').astype(jnp.bfloat16)]
    pallas_call x0 -> x1, Pallas kernels: none -> 299 us  [per_device(): pl.pallas_call(functools.partial(kernel, layers, rows, cols, pieces, r_ti...]
    psum x7 -> x0, waiting for transfers between devices: 285 us -> none  [from_root(): return lax.psum(jnp.where(mine, array, jnp.zeros_like(array)), axis)]
    dot_general x9 -> x0, matrix products: 150 us -> none  [the longest x4 73.1 us: per_device(): lax.dot_general(upward_wide, trans_tile, contract, preferred_element_type...]
    reduce_scatter x4 -> x0, waiting for transfers between devices: 90.5 us -> none  [per_device(): lax.psum_scatter(passed + bounced, 'col', scatter_dimension=0, tiled=True)]
    all_gather x4 -> x0, blocking collectives: 38.7 us -> none  [the longest x3 27.7 us: per_device(): gathered = lax.all_gather(result, 'col', axis=0, tiled=True)]
    ppermute x6 -> x0, waiting for transfers between devices: 13 us -> none  [passed_along(): return lax.ppermute(array, axis, pairs)]
    select_n x7 -> x0, other arithmetic: 10.7 us -> none  [from_root(): return lax.psum(jnp.where(mine, array, jnp.zeros_like(array)), axis)]
  transfers between devices with their start and end apart: 17 -> 0, of which waited for: 16 -> 0; matrix products, arithmetic and copies ran while one was open for 0% -> 0% of each run, Pallas kernels for 0% -> 0%
where the time goes in v1:
time: 307 us; the launch traced here: 303 us
  Pallas kernels  299 us (97%)
  local copies, waits for them, and re-layouts  3.61 us (1%)
    pallas_call x1, Pallas kernels, per_device(): pl.pallas_call(functools.partial(kernel, layers, rows, cols, pieces, r_ti...  299 us

profile of v1, /device:TPU:0, one launch (start us, length us, event | category | flops | bytes accessed | tf_op | source)
XLA Modules:
  0.0 303.1 jit_solution(15120426491491558667)
XLA Ops:
  0.0 1.2 reshape.4
  1.2 0.7 copy.6
  1.9 299.4 %shard_map.37 = bf16[48,3072]{1,0:T(8,128)(2,1)} custom-call(bf16[4,48,768]{2,1,0:T(8,128)(2,1)} %bitcast.8, bf16[3072,6144]{1,0:T(8,128)(2,1)} %bitcast.6, bf16[3072,6144]{1,0:T(8,128)(2,1)} %bitcast.7), custom_call_target="tpu_custom_call" | custom-call | tf_op jit(solution)/shard_map/pallas_call | solution.py:360
  301.4 1.7 copy.8

commit v2 on v1

v2 whole, which is shorter than its diff:
```python
import functools

import jax
import jax.numpy as jnp
from jax import lax
from jax.experimental import pallas as pl
from jax.experimental.pallas import tpu as pltpu
from jax.sharding import PartitionSpec as P

MESH = pl.DeviceIdType.MESH
BF16 = jnp.bfloat16
F32 = jnp.float32


def kernel(
    layers, rows, cols, pieces, r_tile,
    src_ref, trans_ref, refl_ref, out_ref,
    tv, rbuf, sall, nin, incn, pbuf, ybuf, zbuf, natd, natu, ginc, gup, acc, ubuf, urec,
    t_sem, r_sem, s_send, s_recv, n_send, n_recv, y_send, y_recv, z_send, z_recv,
    g_send, g_recv, u_send, u_recv, go_sem,
):
    ratio = rows // cols
    chunks = ratio * pieces
    lay, row, col = (lax.axis_index(name) for name in ("layer", "row", "col"))
    part, cw = natd.shape[1], natd.shape[2]
    traces = cols * part
    tiles = acc.shape[0]
    last = layers - 1
    home_col, home_b = lax.div(row, ratio), lax.rem(row, ratio)

    def other(index, by, size):
        return lax.rem(index + by, size)

    def remote(src, dst, send, recv, target):
        return pltpu.make_async_remote_copy(
            src_ref=src, dst_ref=dst, send_sem=send, recv_sem=recv,
            device_id=target, device_id_type=MESH,
        )

    def column_block(step):
        return lax.rem(step, ratio) * pieces + lax.div(step, ratio)

    def t_copy(j):
        start = pl.multiple_of(j * cw, 128)
        return pltpu.make_async_copy(trans_ref.at[:, pl.ds(start, cw)], tv.at[j], t_sem.at[j])

    def r_copy(step):
        start = pl.multiple_of(column_block(step) * cw, 128)
        slot = lax.rem(step, 2)
        return pltpu.make_async_copy(
            refl_ref.at[:, pl.ds(start, cw)], rbuf.at[slot], r_sem.at[slot]
        )

    def copy_src(c):
        return remote(sall.at[col], sall.at[col], s_send.at[c], s_recv.at[col], (lay, row, c))

    def got_src(c):
        return remote(sall.at[c], sall.at[c], s_send.at[c], s_recv.at[c], (lay, row, c))

    def copy_next(c, p):
        return remote(natd.at[p], nin.at[col, p], n_send.at[c, p], n_recv.at[col, p],
                      (lax.min(lay + 1, last), row, c))

    def got_next(c, p):
        return remote(natd.at[p], nin.at[c, p], n_send.at[c, p], n_recv.at[c, p],
                      (lax.max(lay - 1, 0), row, c))

    def copy_y(c, j):
        return remote(pbuf.at[j, c], ybuf.at[col, j], y_send.at[c, j], y_recv.at[col, j],
                      (lay, row, c))

    def got_y(c, j):
        return remote(pbuf.at[j, c], ybuf.at[c, j], y_send.at[c, j], y_recv.at[c, j],
                      (lay, row, c))

    def copy_z(c, j, own):
        block = pbuf.at[j, col] if own else ybuf.at[c, j]
        goal = ratio * c + lax.div(j, pieces)
        return goal, block, remote(
            block, zbuf.at[row, lax.rem(j, pieces)], z_send.at[c, j],
            z_recv.at[row, lax.rem(j, pieces)], (lay, goal, col),
        )

    def got_z(r, p):
        return remote(natd.at[p], zbuf.at[r, p], z_send.at[0, 0], z_recv.at[r, p],
                      (lay, r, col))

    def copy_g(which, p, r):
        block = incn.at[p, col] if which == 0 else (natd, natu)[which - 1].at[p]
        buf, slot = (ginc, 0) if which == 0 else (gup, 1)
        target = lax.max(lay - 1, 0) if which == 2 else lay
        return block, buf, remote(
            block, buf.at[home_b, p, col], g_send.at[which, p, r],
            g_recv.at[slot, p, home_b, col], (target, r, home_col),
        )

    def got_g(slot, p, b, c):
        buf = gup if slot else ginc
        return remote(natd.at[p], buf.at[b, p, c], g_send.at[0, 0, 0],
                      g_recv.at[slot, p, b, c], (lay, ratio * col + b, c))

    def send_g(which, p):
        for d in range(1, rows):
            copy_g(which, p, other(row, d, rows))[2].start()
        block, buf, copy = copy_g(which, p, row)
        if which == 2:
            copy.start()
            return

        @pl.when(home_col == col)
        def _():
            buf[home_b, p, col] = block[...]

        @pl.when(home_col != col)
        def _():
            copy.start()

    def sent_g(which, p):
        for d in range(1, rows):
            copy_g(which, p, other(row, d, rows))[2].wait_send()
        copy = copy_g(which, p, row)[2]
        if which == 2:
            copy.wait_send()
            return

        @pl.when(home_col != col)
        def _():
            copy.wait_send()

    def arrived_g(slot, p, b):
        for c in range(cols):
            mine = (ratio * col + b == row) & (col == c)
            if slot:
                mine = mine & (lay == last)

            @pl.when(jnp.logical_not(mine))
            def _():
                got_g(slot, p, b, c).wait_recv()

    def copy_u(c, p):
        return remote(ubuf.at[c, p], urec.at[col, p], u_send.at[c, p], u_recv.at[col, p],
                      (lay, row, c))

    def got_u(c, p):
        return remote(ubuf.at[c, p], urec.at[c, p], u_send.at[c, p], u_recv.at[c, p],
                      (lay, row, c))

    for step in range(chunks):
        t_copy((step % ratio) * pieces + step // ratio).start()

    barrier = pltpu.get_barrier_semaphore()

    def greet(target):
        pl.semaphore_signal(barrier, inc=1, device_id=target, device_id_type=MESH)

    for dr in range(rows):
        for dc in range(cols):
            if dr or dc:
                greet((lay, other(row, dr, rows), other(col, dc, cols)))

    @pl.when(lay > 0)
    def _():
        for r in range(rows):
            for c in range(cols):
                greet((lay - 1, r, c))

    @pl.when(lay < last)
    def _():
        for r in range(rows):
            for c in range(cols):
                greet((lay + 1, r, c))

    near = (lay > 0).astype(jnp.int32) + (lay < last).astype(jnp.int32)
    pl.semaphore_wait(barrier, rows * cols - 1 + rows * cols * near)

    for p in range(pieces):
        sall[col, p] = src_ref[:, p * cw:(p + 1) * cw]
    for d in range(1, cols):
        copy_src(other(col, d, cols)).start()
    for step in range(2):
        r_copy(step).start()
    acc[...] = jnp.zeros_like(acc)
    for d in range(1, cols):
        got_src(other(col, d, cols)).wait_recv()

    @pl.when(lay == 0)
    def _():
        for p in range(pieces):
            incn[p] = sall[:, p]

    @pl.when(lay > 0)
    def _():
        for p in range(pieces):
            for c in range(cols):
                got_next(c, p).wait_recv()
            incn[p] = (nin[:, p].astype(F32) + sall[:, p].astype(F32)).astype(BF16)

    def to_row(c, j, own):
        goal, block, copy = copy_z(c, j, own)

        @pl.when(goal == row)
        def _():
            zbuf[row, lax.rem(j, pieces)] = block[...]

        @pl.when(goal != row)
        def _():
            copy.start()

    def forward(j):
        for d in range(1, cols):
            c = other(col, d, cols)
            got_y(c, j).wait_recv()
            to_row(c, j, False)

    def down_step(step, carry):
        j = column_block(step)
        t_copy(j).wait()
        total = jnp.zeros((traces, cw), F32)
        for p in range(pieces):
            total += jnp.dot(
                incn[p].reshape(traces, cw), tv[j, pl.ds(p * cw, cw), :],
                preferred_element_type=F32,
            )
        pbuf[j] = total.astype(BF16).reshape(cols, part, cw)
        for d in range(1, cols):
            copy_y(other(col, d, cols), j).start()
        to_row(col, j, True)

        @pl.when(step > 0)
        def _():
            forward(column_block(step - 1))

        return carry

    lax.fori_loop(0, chunks, down_step, 0)
    forward(column_block(chunks - 1))

    @pl.when(lay == last)
    def _():
        for p in range(pieces):
            send_g(0, p)

    for p in range(pieces):
        for d in range(1, rows):
            got_z(other(row, d, rows), p).wait_recv()
        natd[p] = jnp.sum(zbuf[:, p].astype(F32), axis=0).astype(BF16)

        @pl.when(lay < last)
        def _():
            for c in range(cols):
                copy_next(c, p).start()

        @pl.when(lay == last)
        def _():
            send_g(1, p)

    def signal_go():
        pl.semaphore_signal(
            go_sem, inc=1, device_id=(lay - 1, row, col), device_id_type=MESH
        )

    @pl.when((lay > 0) & (lay < last))
    def _():
        signal_go()

    @pl.when(lay < last)
    def _():
        early = pieces // 2
        for p in range(early):
            send_g(0, p)
        pl.semaphore_wait(go_sem, 1)
        for p in range(early, pieces):
            send_g(0, p)

    contract = (((1,), (1,)), ((), ()))

    def times(lhs, rhs):
        return lax.dot_general(lhs, rhs, contract, preferred_element_type=F32)

    def add_product(lhs, weights):
        for i in range(tiles):
            acc[i] += times(lhs, weights[pl.ds(i * r_tile, r_tile), :])

    def reflect_step(step, carry):
        b, p = lax.rem(step, ratio), lax.div(step, ratio)
        arrived_g(0, p, b)
        r_copy(step).wait()
        add_product(ginc[b, p].reshape(traces, cw), rbuf.at[lax.rem(step, 2)])

        @pl.when(step + 2 < chunks)
        def _():
            r_copy(step + 2).start()

        return carry

    lax.fori_loop(0, chunks, reflect_step, 0)

    def up_step(step, carry):
        b, p = lax.rem(step, ratio), lax.div(step, ratio)
        arrived_g(1, p, b)
        add_product(gup[b, p].reshape(traces, cw), tv.at[b * pieces + p])
        return carry

    lax.fori_loop(0, chunks - ratio, up_step, 0)
    end = pieces - 1
    for b in range(ratio):
        arrived_g(1, end, b)

    @pl.when((lay > 0) & (lay == last))
    def _():
        signal_go()

    per = cw // r_tile

    def piece_of(p, c):
        found = []
        for i in range(per):
            found.append(acc[p * per + i, pl.ds(pl.multiple_of(c * part, 8), part), :])
        return jnp.concatenate(found, axis=1)

    for p in range(pieces):
        for i in range(p * per, (p + 1) * per):
            total = acc[i]
            for b in range(ratio):
                total += times(
                    gup[b, end].reshape(traces, cw),
                    tv[b * pieces + end, pl.ds(i * r_tile, r_tile), :],
                )
            acc[i] = total
        for d in range(1, cols):
            c = other(col, d, cols)
            ubuf[c, p] = piece_of(p, c).astype(BF16)
            copy_u(c, p).start()

    for p in range(pieces):
        total = piece_of(p, col)
        for d in range(1, cols):
            c = other(col, d, cols)
            got_u(c, p).wait_recv()
            total += urec[c, p].astype(F32)
        result = total.astype(BF16)
        natu[p] = result
        out_ref[:, p * cw:(p + 1) * cw] = result

        @pl.when(lay > 0)
        def _():
            send_g(2, p)

    for d in range(1, cols):
        c = other(col, d, cols)
        copy_src(c).wait_send()
        for p in range(pieces):
            copy_u(c, p).wait_send()
        for j in range(chunks):
            copy_y(c, j).wait_send()
    for d in range(cols):
        c = other(col, d, cols)
        for j in range(chunks):
            goal, _, copy = copy_z(c, j, d == 0)

            @pl.when(goal != row)
            def _():
                copy.wait_send()

    for p in range(pieces):
        sent_g(0, p)

        @pl.when(lay < last)
        def _():
            for c in range(cols):
                copy_next(c, p).wait_send()

        @pl.when(lay == last)
        def _():
            sent_g(1, p)

        @pl.when(lay > 0)
        def _():
            sent_g(2, p)


def split_of(width):
    for pieces in (4, 3, 2):
        if width % (pieces * 128) == 0:
            return pieces
    return 1


def per_device(layers, rows, cols, sources, transmission, reflection):
    ratio = rows // cols
    own, width = sources.shape[1], sources.shape[2]
    part = -(-own // 16) * 16
    pieces = split_of(width)
    cw = width // pieces
    chunks = ratio * pieces
    r_tile = 256 if cw % 256 == 0 else 128
    traces = cols * part
    src = jnp.pad(sources[0], ((0, part - own), (0, 0)))
    dma, vmem = pltpu.SemaphoreType.DMA, pltpu.VMEM
    result = pl.pallas_call(
        functools.partial(kernel, layers, rows, cols, pieces, r_tile),
        out_shape=jax.ShapeDtypeStruct((part, width), BF16),
        in_specs=[
            pl.BlockSpec(memory_space=pltpu.VMEM),
            pl.BlockSpec(memory_space=pl.ANY),
            pl.BlockSpec(memory_space=pl.ANY),
        ],
        out_specs=pl.BlockSpec(memory_space=pltpu.VMEM),
        scratch_shapes=[
            vmem((chunks, width, cw), BF16),
            vmem((2, width, cw), BF16),
            vmem((cols, pieces, part, cw), BF16),
            vmem((cols, pieces, part, cw), BF16),
            vmem((pieces, cols, part, cw), BF16),
            vmem((chunks, cols, part, cw), BF16),
            vmem((cols, chunks, part, cw), BF16),
            vmem((rows, pieces, part, cw), BF16),
            vmem((pieces, part, cw), BF16),
            vmem((pieces, part, cw), BF16),
            vmem((ratio, pieces, cols, part, cw), BF16),
            vmem((ratio, pieces, cols, part, cw), BF16),
            vmem((width // r_tile, traces, r_tile), F32),
            vmem((cols, pieces, part, cw), BF16),
            vmem((cols, pieces, part, cw), BF16),
            dma((chunks,)), dma((2,)),
            dma((cols,)), dma((cols,)),
            dma((cols, pieces)), dma((cols, pieces)),
            dma((cols, chunks)), dma((cols, chunks)),
            dma((cols, chunks)), dma((rows, pieces)),
            dma((3, pieces, rows)), dma((2, pieces, ratio, cols)),
            dma((cols, pieces)), dma((cols, pieces)),
            pltpu.SemaphoreType.REGULAR,
        ],
        compiler_params=pltpu.CompilerParams(
            collective_id=0, has_side_effects=True, vmem_limit_bytes=66_000_000
        ),
    )(src, transmission[0], reflection[0])
    return result[None, :own]


def solution(mesh):
    sizes = [mesh.shape[name] for name in ("layer", "row", "col")]
    return jax.shard_map(
        functools.partial(per_device, *sizes),
        mesh=mesh,
        in_specs=(P("layer", "col", "row"), P("layer", "row", "col"), P("layer", "row", "col")),
        out_specs=P("layer", "col", "row"),
        check_vma=False,
    )
```

time: 307 us -> 219 us (0.71); the launches traced: 303 us -> 218 us
  Pallas kernels: 299 us -> 217 us
    pallas_call x1, Pallas kernels: 299 us -> 217 us  [per_device(): pl.pallas_call(functools.partial(kernel, layers, rows, cols, pieces, r_ti...]
where the time goes in v2:
time: 219 us; the launch traced here: 218 us
  Pallas kernels  217 us (99%)
    pallas_call x1, Pallas kernels, per_device(): pl.pallas_call(functools.partial(kernel, layers, rows, cols, pieces, r_ti...  217 us

profile of v2, /device:TPU:0, one launch (start us, length us, event | category | flops | bytes accessed | tf_op | source)
XLA Modules:
  0.0 218.3 jit_solution(11591830992735207311)
XLA Ops:
  0.0 216.6 %shard_map.37 = bf16[48,3072]{1,0:T(8,128)(2,1)} custom-call(bf16[48,3072]{1,0:T(8,128)(2,1)} %bitcast.7, bf16[3072,6144]{1,0:T(8,128)(2,1)} %bitcast.4, bf16[3072,6144]{1,0:T(8,128)(2,1)} %bitcast.5), custom_call_target="tpu_custom_call" | custom-call | tf_op jit(solution)/shard_map/pallas_call | solution.py:400
  216.6 1.7 copy.5

commit v3 on v2

--- a/solution.py
+++ b/solution.py
@@ -15,9 +15,9 @@
 def kernel(
     layers, rows, cols, pieces, r_tile,
     src_ref, trans_ref, refl_ref, out_ref,
-    tv, rbuf, sall, nin, incn, pbuf, ybuf, zbuf, natd, natu, ginc, gup, acc, ubuf, urec,
+    tv, rbuf, sall, nin, incn, pbuf, ybuf, zbuf, natd, natu, lent, ginc, gup, acc, ubuf, urec,
     t_sem, r_sem, s_send, s_recv, n_send, n_recv, y_send, y_recv, z_send, z_recv,
-    g_send, g_recv, u_send, u_recv, go_sem,
+    g_send, g_recv, u_send, u_recv, l_send, l_recv,
 ):
     ratio = rows // cols
     chunks = ratio * pieces
@@ -26,6 +26,9 @@
     traces = cols * part
     tiles = acc.shape[0]
     last = layers - 1
+    half = layers // 2
+    helper = lax.rem(lay + half, layers)
+    helped = lax.rem(lay + layers - half, layers)
     home_col, home_b = lax.div(row, ratio), lax.rem(row, ratio)
 
     def other(index, by, size):
@@ -86,9 +89,9 @@
                       (lay, r, col))
 
     def copy_g(which, p, r):
-        block = incn.at[p, col] if which == 0 else (natd, natu)[which - 1].at[p]
+        block = (lent, natd, natu)[which].at[p]
         buf, slot = (ginc, 0) if which == 0 else (gup, 1)
-        target = lax.max(lay - 1, 0) if which == 2 else lay
+        target = (helped, lay, lax.max(lay - 1, 0))[which]
         return block, buf, remote(
             block, buf.at[home_b, p, col], g_send.at[which, p, r],
             g_recv.at[slot, p, home_b, col], (target, r, home_col),
@@ -99,11 +102,15 @@
         return remote(natd.at[p], buf.at[b, p, c], g_send.at[0, 0, 0],
                       g_recv.at[slot, p, b, c], (lay, ratio * col + b, c))
 
+    def copy_l(p, target):
+        return remote(incn.at[p, col], lent.at[p], l_send.at[p], l_recv.at[p],
+                      (target, row, col))
+
     def send_g(which, p):
         for d in range(1, rows):
             copy_g(which, p, other(row, d, rows))[2].start()
         block, buf, copy = copy_g(which, p, row)
-        if which == 2:
+        if which != 1:
             copy.start()
             return
 
@@ -119,7 +126,7 @@
         for d in range(1, rows):
             copy_g(which, p, other(row, d, rows))[2].wait_send()
         copy = copy_g(which, p, row)[2]
-        if which == 2:
+        if which != 1:
             copy.wait_send()
             return
 
@@ -129,9 +136,10 @@
 
     def arrived_g(slot, p, b):
         for c in range(cols):
-            mine = (ratio * col + b == row) & (col == c)
-            if slot:
-                mine = mine & (lay == last)
+            if slot == 0:
+                got_g(slot, p, b, c).wait_recv()
+                continue
+            mine = (ratio * col + b == row) & (col == c) & (lay == last)
 
             @pl.when(jnp.logical_not(mine))
             def _():
@@ -153,25 +161,20 @@
     def greet(target):
         pl.semaphore_signal(barrier, inc=1, device_id=target, device_id_type=MESH)
 
-    for dr in range(rows):
-        for dc in range(cols):
-            if dr or dc:
-                greet((lay, other(row, dr, rows), other(col, dc, cols)))
-
-    @pl.when(lay > 0)
-    def _():
-        for r in range(rows):
-            for c in range(cols):
-                greet((lay - 1, r, c))
-
-    @pl.when(lay < last)
-    def _():
-        for r in range(rows):
-            for c in range(cols):
-                greet((lay + 1, r, c))
-
-    near = (lay > 0).astype(jnp.int32) + (lay < last).astype(jnp.int32)
-    pl.semaphore_wait(barrier, rows * cols - 1 + rows * cols * near)
+    def greet_all(step, carry):
+        r, c = lax.div(step, cols), lax.rem(step, cols)
+        for d in range(layers):
+            l = other(lay, d, layers)
+            if d:
+                greet((l, r, c))
+            else:
+                @pl.when((r != row) | (c != col))
+                def _():
+                    greet((l, r, c))
+        return carry
+
+    lax.fori_loop(0, rows * cols, greet_all, 0)
+    pl.semaphore_wait(barrier, layers * rows * cols - 1)
 
     for p in range(pieces):
         sall[col, p] = src_ref[:, p * cw:(p + 1) * cw]
@@ -183,10 +186,20 @@
     for d in range(1, cols):
         got_src(other(col, d, cols)).wait_recv()
 
+    def relay():
+        for p in range(pieces):
+            copy_l(p, helped).wait_recv()
+            send_g(0, p)
+
     @pl.when(lay == 0)
     def _():
         for p in range(pieces):
             incn[p] = sall[:, p]
+            copy_l(p, helper).start()
+
+    @pl.when(lay >= half)
+    def _():
+        relay()
 
     @pl.when(lay > 0)
     def _():
@@ -194,6 +207,7 @@
             for c in range(cols):
                 got_next(c, p).wait_recv()
             incn[p] = (nin[:, p].astype(F32) + sall[:, p].astype(F32)).astype(BF16)
+            copy_l(p, helper).start()
 
     def to_row(c, j, own):
         goal, block, copy = copy_z(c, j, own)
@@ -235,11 +249,6 @@
     lax.fori_loop(0, chunks, down_step, 0)
     forward(column_block(chunks - 1))
 
-    @pl.when(lay == last)
-    def _():
-        for p in range(pieces):
-            send_g(0, p)
-
     for p in range(pieces):
         for d in range(1, rows):
             got_z(other(row, d, rows), p).wait_recv()
@@ -254,23 +263,9 @@
         def _():
             send_g(1, p)
 
-    def signal_go():
-        pl.semaphore_signal(
-            go_sem, inc=1, device_id=(lay - 1, row, col), device_id_type=MESH
-        )
-
-    @pl.when((lay > 0) & (lay < last))
+    @pl.when(lay < half)
     def _():
-        signal_go()
-
-    @pl.when(lay < last)
-    def _():
-        early = pieces // 2
-        for p in range(early):
-            send_g(0, p)
-        pl.semaphore_wait(go_sem, 1)
-        for p in range(early, pieces):
-            send_g(0, p)
+        relay()
 
     contract = (((1,), (1,)), ((), ()))
 
@@ -305,10 +300,6 @@
     end = pieces - 1
     for b in range(ratio):
         arrived_g(1, end, b)
-
-    @pl.when((lay > 0) & (lay == last))
-    def _():
-        signal_go()
 
     per = cw // r_tile
 
@@ -363,6 +354,7 @@
                 copy.wait_send()
 
     for p in range(pieces):
+        copy_l(p, helper).wait_send()
         sent_g(0, p)
 
         @pl.when(lay < last)
@@ -417,6 +409,7 @@
             vmem((rows, pieces, part, cw), BF16),
             vmem((pieces, part, cw), BF16),
             vmem((pieces, part, cw), BF16),
+            vmem((pieces, part, cw), BF16),
             vmem((ratio, pieces, cols, part, cw), BF16),
             vmem((ratio, pieces, cols, part, cw), BF16),
             vmem((width // r_tile, traces, r_tile), F32),
@@ -429,7 +422,7 @@
             dma((cols, chunks)), dma((rows, pieces)),
             dma((3, pieces, rows)), dma((2, pieces, ratio, cols)),
             dma((cols, pieces)), dma((cols, pieces)),
-            pltpu.SemaphoreType.REGULAR,
+            dma((pieces,)), dma((pieces,)),
         ],
         compiler_params=pltpu.CompilerParams(
             collective_id=0, has_side_effects=True, vmem_limit_bytes=66_000_000

time: 219 us -> 225 us (1.027)
  Pallas kernels: 217 us -> 222 us
    pallas_call x1, Pallas kernels: 217 us -> 222 us  [per_device(): pl.pallas_call(functools.partial(kernel, layers, rows, cols, pieces, r_ti...]
where the time goes in v3:
time: 225 us; the launch traced here: 224 us
  Pallas kernels  222 us (99%)
    pallas_call x1, Pallas kernels, per_device(): pl.pallas_call(functools.partial(kernel, layers, rows, cols, pieces, r_ti...  222 us

profile of v3, /device:TPU:0, one launch (start us, length us, event | category | flops | bytes accessed | tf_op | source)
XLA Modules:
  0.0 223.7 jit_solution(16514363979923675523)
XLA Ops:
  0.0 222.0 %shard_map.37 = bf16[48,3072]{1,0:T(8,128)(2,1)} custom-call(bf16[48,3072]{1,0:T(8,128)(2,1)} %bitcast.7, bf16[3072,6144]{1,0:T(8,128)(2,1)} %bitcast.4, bf16[3072,6144]{1,0:T(8,128)(2,1)} %bitcast.5), custom_call_target="tpu_custom_call" | custom-call | tf_op jit(solution)/shard_map/pallas_call | solution.py:392
  222.0 1.7 copy.5

commit v4 on v3

--- a/solution.py
+++ b/solution.py
@@ -180,8 +180,6 @@
         sall[col, p] = src_ref[:, p * cw:(p + 1) * cw]
     for d in range(1, cols):
         copy_src(other(col, d, cols)).start()
-    for step in range(2):
-        r_copy(step).start()
     acc[...] = jnp.zeros_like(acc)
     for d in range(1, cols):
         got_src(other(col, d, cols)).wait_recv()
@@ -195,7 +193,6 @@
     def _():
         for p in range(pieces):
             incn[p] = sall[:, p]
-            copy_l(p, helper).start()
 
     @pl.when(lay >= half)
     def _():
@@ -207,7 +204,6 @@
             for c in range(cols):
                 got_next(c, p).wait_recv()
             incn[p] = (nin[:, p].astype(F32) + sall[:, p].astype(F32)).astype(BF16)
-            copy_l(p, helper).start()
 
     def to_row(c, j, own):
         goal, block, copy = copy_z(c, j, own)
@@ -248,6 +244,10 @@
 
     lax.fori_loop(0, chunks, down_step, 0)
     forward(column_block(chunks - 1))
+    for p in range(pieces):
+        copy_l(p, helper).start()
+    for step in range(2):
+        r_copy(step).start()
 
     for p in range(pieces):
         for d in range(1, rows):

time: 225 us -> 225 us (level)
  no operation moved by 1% of the time
where the time goes in v4:
time: 225 us; the launch traced here: 224 us
  Pallas kernels  222 us (99%)
    pallas_call x1, Pallas kernels, per_device(): pl.pallas_call(functools.partial(kernel, layers, rows, cols, pieces, r_ti...  222 us

profile of v4, /device:TPU:0, one launch (start us, length us, event | category | flops | bytes accessed | tf_op | source)
XLA Modules:
  0.0 224.2 jit_solution(16931169429009496998)
XLA Ops:
  0.0 222.5 %shard_map.37 = bf16[48,3072]{1,0:T(8,128)(2,1)} custom-call(bf16[48,3072]{1,0:T(8,128)(2,1)} %bitcast.7, bf16[3072,6144]{1,0:T(8,128)(2,1)} %bitcast.4, bf16[3072,6144]{1,0:T(8,128)(2,1)} %bitcast.5), custom_call_target="tpu_custom_call" | custom-call | tf_op jit(solution)/shard_map/pallas_call | solution.py:392
  222.5 1.7 copy.5
